TPU v7x, 32 devices: a whole 2x2x4 slice. The times are simulated.
32 devices in a mesh: group: 1, path: 32 (over z, y, x, core).
Axes of the slice: x: 2, y: 2, z: 4, core: 2. Of those that a mesh axis runs over, the one named last changes fastest.
Arguments:
- normals: float32 [8, 32, 8192], P(None, None, ('group', 'path')), may hold values from -6 to 6
- start_state: float32 [32, 8192], P(None, ('group', 'path')), may hold values from -0.12 to 0.12
- later_adjoint: float32 [32, 8192], P(None, ('group', 'path')), may hold values from -1.8 to 1.8
- vol: float32 [8], replicated, may hold values from 0.004 to 0.016
- factor_load: float32 [32, 960], replicated, may hold values from -2.1 to 2.1
- knots: float32 [960], replicated, may hold values from 0.01 to 0.05
- spline_jac: float32 [960, 960], replicated
- cashflows: bfloat16 [256, 960], P(('group', 'path')), may hold values from -0.1875 to 0.1875
- trade_set: int32 [256, 1], P(('group', 'path')), may hold values from 0 to 127
- trade_end: int32 [256], P(('group', 'path')), may hold values from 240 to 960
- set_cpty: int32 [128, 1], P('group'), may hold values from 0 to 63
- default_prob: float32 [8, 64], replicated, may hold values from 0.01 to 0.1
- base_value: float32 [8, 128], P(None, 'group'), may hold values from -3 to 3
Outputs:
- knot_grad: float32 [960], P('group')
- alloc: float32 [256], P(('group', 'path'))
- start_adjoint: float32 [32, 8192], P(None, ('group', 'path'))
All inputs are finite; a program needn't handle non-finite values.
Results may differ from a plain program's by a relative error of at most 0.0011.
Values may be sent and summed in bfloat16 or wider, within the bound.
No kernel may reach another device: no remote copies, remote signals or barrier semaphores. Data moves between devices by JAX's collectives and lax.ppermute only.
A program may use at most 64 MiB of HBM per device.

v0:
```python
import math
import jax
import jax.numpy as jnp
from jax import lax
from jax.sharding import PartitionSpec as P

MEAN_REV = 0.05
STEP_YEARS = 0.25
HORIZON_YEARS = 30.0
SHARPNESS = 4.0
LOSS_RATE = 0.6


def curve_terms(knots, spline_jac, date_count, knot_count):
    zero_rate = jnp.dot(spline_jac, knots, precision=lax.Precision.HIGHEST)
    knot_index = jnp.arange(knot_count, dtype=jnp.int32)
    date_index = jnp.arange(date_count, dtype=jnp.int32)
    is_alive = 120 * (knot_index[None, :] + 1) > knot_count * (date_index[:, None] + 1)
    maturity = HORIZON_YEARS * (knot_index + 1).astype(jnp.float32) / knot_count
    fixing = STEP_YEARS * (date_index + 1).astype(jnp.float32)
    horizon = jnp.where(is_alive, maturity[None, :] - fixing[:, None], jnp.float32(0.0))
    loading = (1.0 - jnp.exp(-MEAN_REV * horizon)) / MEAN_REV
    discount = jnp.where(is_alive, jnp.exp(-zero_rate[None, :] * horizon), jnp.float32(0.0))
    return (horizon, loading, discount)


def state_path(start_state, vol, normals):
    decay_factor = math.exp(-MEAN_REV * STEP_YEARS)
    state = start_state
    collected = []
    for index in range(normals.shape[0]):
        state = decay_factor * state + vol[index] * normals[index]
        collected.append(state)
    return jnp.stack(collected)


def per_device(
    normals,
    start_state,
    later_adjoint,
    vol,
    factor_load,
    knots,
    spline_jac,
    cashflows,
    trade_set,
    trade_end,
    set_cpty,
    default_prob,
    base_value,
):
    highest = lax.Precision.HIGHEST
    date_count = normals.shape[0]
    knot_count = knots.shape[0]
    set_count = base_value.shape[1]
    paths_all = normals.shape[2] * lax.axis_size("path")
    horizon, loading, discount = curve_terms(knots, spline_jac, date_count, knot_count)
    knot_index = jnp.arange(knot_count, dtype=jnp.int32)
    live_flows = jnp.where(
        knot_index[None, :] < trade_end[:, None], cashflows, jnp.zeros_like(cashflows)
    )
    set_ids = trade_set[:, 0]
    labels = jnp.arange(set_count, dtype=jnp.int32)
    all_flows, all_sets = (
        lax.all_gather(live_flows, "path", axis=0, tiled=True),
        lax.all_gather(set_ids, "path", axis=0, tiled=True),
    )
    member = (labels[:, None] == all_sets[None, :]).astype(jnp.bfloat16)
    net_flows = jnp.dot(member, all_flows, preferred_element_type=jnp.float32).astype(jnp.bfloat16)
    counter = (
        jnp.arange(default_prob.shape[1], dtype=jnp.int32)[:, None] == set_cpty[:, 0][None, :]
    ).astype(jnp.float32)
    weight = LOSS_RATE * jnp.dot(default_prob, counter, precision=highest)
    states = state_path(start_state, vol, normals)
    shift = jnp.einsum("fm,ifp->imp", factor_load, states, precision=highest)
    bond_term = jnp.exp(-loading[:, :, None] * shift)
    feat_exact = discount[:, :, None] * bond_term
    features = feat_exact.astype(jnp.bfloat16)
    values = jnp.einsum("nm,imp->inp", net_flows, features, preferred_element_type=jnp.float32)
    mean_value = lax.psum(jnp.sum(values, axis=2), "path") / paths_all
    shifted = values - mean_value[:, :, None] + base_value[:, :, None]
    slope = weight[:, :, None] * jax.nn.sigmoid(SHARPNESS * shifted)
    mean_slope = lax.psum(jnp.sum(slope, axis=2), "path") / paths_all
    set_adjoint = (slope - mean_slope[:, :, None]).astype(jnp.bfloat16)
    feat_adjoint = jnp.einsum(
        "nm,inp->imp", net_flows, set_adjoint, preferred_element_type=jnp.float32
    )
    state_local = -jnp.einsum(
        "fm,imp->ifp",
        factor_load,
        feat_adjoint * feat_exact * loading[:, :, None],
        precision=highest,
    )
    discount_grad = jnp.sum(feat_adjoint * bond_term, axis=2)
    rate_adjoint = -jnp.sum(discount_grad * discount * horizon, axis=0) / paths_all
    rate_total = lax.psum(rate_adjoint, "path")
    knot_grad = jnp.dot(spline_jac.T, rate_total, precision=highest)
    load_sums = (
        jnp.einsum("inp,imp->nm", set_adjoint, features, preferred_element_type=jnp.float32)
        / paths_all
    )
    set_rows = load_sums[all_sets]
    trade_part = jnp.sum(all_flows.astype(jnp.float32) * set_rows, axis=1)
    alloc = lax.psum_scatter(trade_part, "path", scatter_dimension=0, tiled=True)
    decay_factor = math.exp(-MEAN_REV * STEP_YEARS)
    carried = later_adjoint + state_local[date_count - 1]
    for index in reversed(range(date_count - 1)):
        carried = state_local[index] + decay_factor * carried
    start_adjoint = decay_factor * carried
    return (knot_grad, alloc, start_adjoint)


def solution(mesh):
    in_specs = (
        P(None, None, ("group", "path")),
        P(None, ("group", "path")),
        P(None, ("group", "path")),
        P(),
        P(),
        P(),
        P(),
        P(("group", "path"), None),
        P(("group", "path"), None),
        P(("group", "path")),
        P("group", None),
        P(),
        P(None, "group"),
    )
    out_specs = (P("group"), P(("group", "path")), P(None, ("group", "path")))
    return jax.shard_map(
        per_device, mesh=mesh, in_specs=in_specs, out_specs=out_specs, check_vma=False
    )
```

profile of v0, /device:TPU:0, one launch (start us, length us, event | category | flops | bytes accessed | tf_op | source)
XLA Modules:
  0.0 270.6 jit_solution(15762425865365894682)
XLA Ops:
  0.6 0.0 copy-start
  0.7 0.8 bitcast_dynamic-update-slice_fusion.8
  1.5 41.9 %all-reduce = s32[256]{0:T(256)S(1)} all-reduce(s32[256]{0:T(256)S(1)} %bitcast_dynamic-update-slice_fusion.8), channel_id=2, replica_groups=mesh['group'=1,'path'=32] {'path'}, use_global_device_ids=true, to_apply=%add | all-reduce | flops 256 | bytes 2048 | tf_op jit(solution)/shard_map/all_gather | solution.py:66
  43.4 0.6 pad_clamp_fusion
  44.0 0.8 fusion.18
  44.8 0.0 copy-start.5
  44.9 0.0 copy-start.7
  44.9 5.4 %fusion.50 = f32[1,960]{1,0:T(1,128)S(1)} fusion(f32[960,960]{1,0:T(8,128)} %param.19, f32[960,1]{0,1:T(1,128)} %bitcast.192), kind=kOutput, calls=%fused_computation.96 | convolution fusion | flops 11059200 | bytes 3694080 | tf_op jit(solution)/shard_map/dot_general | solution.py:15
  50.3 1.6 fusion.48
  52.0 0.8 fusion.42
  52.8 0.7 subtract_multiply_fusion
  53.5 1.5 bitcast_dynamic-update-slice_fusion.7
  54.9 2.0 bitcast_dynamic-update-slice_fusion.6
  57.0 1.5 bitcast_dynamic-update-slice_fusion.5
  58.4 2.0 bitcast_dynamic-update-slice_fusion.4
  60.5 1.5 bitcast_dynamic-update-slice_fusion.3
  61.9 2.1 bitcast_dynamic-update-slice_fusion.2
  64.1 1.4 bitcast_dynamic-update-slice_fusion.1
  65.4 2.1 bitcast_dynamic-update-slice_fusion
  67.5 41.7 %all_gather.7 = bf16[256,960]{1,0:T(8,128)(2,1)S(1)} all-gather(bf16[8,960]{1,0:T(8,128)(2,1)S(1)} %fusion.42), channel_id=1, replica_groups=mesh['group'=1,'path'=32] {'path'}, dimensions={0}, use_global_device_ids=true | all-gather | bytes 506880 | tf_op jit(solution)/shard_map/all_gather | solution.py:65
  109.2 0.3 fusion.17
  109.6 0.0 copy-done
  109.6 0.0 copy-start.13
  109.6 6.5 %fusion.23 = f32[8,256,960]{1,2,0:T(8,128)S(1)} fusion(f32[8,32,256]{2,1,0:T(8,128)S(1)} %bitcast_dynamic-update-slice_fusion, f32[32,960]{1,0:T(8,128)S(1)} %copy-done), kind=kOutput, calls=%fused_computation.28 | convolution fusion | flops 754974720 | bytes 8249344 | tf_op jit(solution)/shard_map/fm,ifp->imp/dot_general | solution.py:75
  116.1 0.0 copy-start.1
  116.1 3.1 %copy-done.1 = f32[8,256,960]{1,2,0:T(8,128)} copy-done((f32[8,256,960]{1,2,0:T(8,128)}, f32[8,256,960]{1,2,0:T(8,128)S(1)}, u32[]{:S(2)}) %copy-start.1) | copy-done | bytes 7864344
  119.1 5.4 %fusion.49 = (f32[8,128]{1,0:T(8,128)S(1)}, f32[8,128,256]{1,2,0:T(8,128)S(1)}) fusion(bf16[128,960,1]{0,1,2:T(8,128)(2,1)S(1)} %fusion.17, f32[8,256,960]{1,2,0:T(8,128)S(1)} %fusion.23, f32[8,960]{1,0:T(8,128)S(1)} %get-tuple-element.12, f32[8,960]{1,0:T(8,128)S(1)} %get-tuple-element.13), kind=kOutput, calls=%fused_computation.95 | convolution fusion | flops 509475840 | bytes 9224192 | tf_op jit(solution)/shard_map/nm,imp->inp/dot_general | solution.py:79
  124.6 37.0 %psum.21 = f32[8,128]{1,0:T(8,128)S(1)} all-reduce(f32[8,128]{1,0:T(8,128)S(1)} %get-tuple-element.22), channel_id=1, replica_groups=mesh['group'=1,'path'=32] {'path'}, use_global_device_ids=true, to_apply=%region_1.2 | all-reduce | flops 1024 | bytes 8192 | tf_op jit(solution)/shard_map/psum | solution.py:80
  161.6 0.0 copy-done.13
  161.6 0.3 fusion.47
  162.0 41.2 %psum.22 = f32[8,128]{1,0:T(8,128)S(1)} all-reduce(f32[8,128]{1,0:T(8,128)S(1)} %fusion.47), channel_id=1, replica_groups=mesh['group'=1,'path'=32] {'path'}, use_global_device_ids=true, to_apply=%region_3.4 | all-reduce | flops 1024 | bytes 8192 | tf_op jit(solution)/shard_map/psum | solution.py:83
  203.1 0.0 copy-done.11
  203.2 0.0 copy-start.15
  203.2 0.6 copy-done.15
  203.8 5.4 %fusion.10 = f32[128,960]{0,1:T(8,128)S(1)} fusion(f32[8,256,960]{1,2,0:T(8,128)} %copy-done.1, f32[8,960]{1,0:T(8,128)S(1)} %get-tuple-element.12, f32[8,960]{1,0:T(8,128)S(1)} %get-tuple-element.13, f32[8,128]{1,0:T(8,128)S(1)} %broadcast_multiply_fusion, f32[8,128,256]{1,2,0:T(8,128)S(1)} %get-tuple-element.23, f32[8,128]{1,0:T(8,128)S(1)} %copy-done.13, ...), kind=kOutput, calls=%fused_computation.16 | convolution fusion | flops 511696896 | bytes 9482240 | tf_op jit(solution)/shard_map/inp,imp->nm/dot_general | solution.py:99
  209.2 0.2 copy.21
  209.4 1.2 gather_fusion
  210.6 0.0 slice-start
  210.6 0.2 multiply_reduce_fusion
  210.8 0.0 copy-start.4
  210.8 6.4 %fusion = (f32[8,960]{1,0:T(8,128)S(1)}, f32[8,256,960]{1,2,0:T(8,128)S(1)}) fusion(f32[8,256,960]{1,2,0:T(8,128)} %copy-done.1, f32[8,960]{1,0:T(8,128)S(1)} %get-tuple-element.12, bf16[128,960,1]{0,1,2:T(8,128)(2,1)S(1)} %fusion.17, f32[8,128]{1,0:T(8,128)} %copy-done.15, f32[8,128]{1,0:T(8,128)} %param.25, f32[8,128,256]{1,2,0:T(8,128)S(1)} %get-tuple-element.23, ...), kind=kOutput, calls=%fused_computation.3 | convolution fusion | flops 511566336 | bytes 17100800 | tf_op jit(solution)/shard_map/nm,inp->imp/dot_general | solution.py:85
  217.3 0.0 copy-start.12
  217.4 7.6 %fusion.14 = f32[8,32,256]{2,1,0:T(8,128)S(1)} fusion(f32[8,256,960]{1,2,0:T(8,128)S(1)} %get-tuple-element.25, f32[8,256,960]{1,2,0:T(8,128)S(1)} %bitcast.190, f32[8,960]{1,0:T(8,128)S(1)} %copy-done.4, f32[8,960]{1,0:T(8,128)S(1)} %get-tuple-element.12, f32[8,960]{1,0:T(8,128)S(1)} %copy-done.3, f32[32,960]{1,0:T(8,128)S(1)} %copy-done), kind=kOutput, calls=%fused_computation.19 | convolution fusion | flops 762904576 | bytes 16205824 | tf_op jit(solution)/shard_map/fm,imp->ifp/dot_general | solution.py:88
  225.0 0.6 fusion.41
  225.6 0.1 multiply_reduce_fusion.1
  225.7 39.6 %all-reduce.2 = (f32[960]{0:T(1024)S(1)}, f32[256]{0:T(256)S(1)}) all-reduce(f32[960]{0:T(1024)S(1)} %negate_multiply_fusion, f32[256]{0:T(256)S(1)} %multiply_reduce_fusion), channel_id=1, replica_groups=mesh['group'=1,'path'=32] {'path'}, use_global_device_ids=true, to_apply=%region_6.7 | all-reduce | flops 1216 | bytes 9728 | tf_op jit(solution)/shard_map/psum | solution.py:96
  265.3 4.7 %fusion.5 = f32[1,960]{1,0:T(1,128)} fusion(f32[960,1]{0,1:T(1,128)S(1)} %bitcast.194, f32[960,960]{1,0:T(8,128)} %param.19), kind=kOutput, calls=%fused_computation.9 | convolution fusion | flops 11059200 | bytes 3694080 | tf_op jit(solution)/shard_map/dot_general | solution.py:97
  270.0 0.6 dynamic-slice
  (41 shorter events, 0.1 us)
Async XLA Ops:
  0.6 108.9 %copy-start = (f32[32,960]{1,0:T(8,128)S(1)}, f32[32,960]{1,0:T(8,128)}, u32[]{:S(2)}) copy-start(f32[32,960]{1,0:T(8,128)} %param.17) | copy-start | bytes 368644
  0.7 123.9 %copy-start.16 = (s32[8]{0:T(128)}, s32[8]{0:T(128)S(1)}, u32[]{:S(2)}) copy-start(s32[8]{0:T(128)S(1)} %fusion.46) | copy-start | bytes 100
  0.7 123.9 %copy-start.18 = (f32[8]{0:T(128)}, f32[8]{0:T(128)S(1)}, u32[]{:S(2)}) copy-start(f32[8]{0:T(128)S(1)} %convert_multiply_fusion.1) | copy-start | bytes 100
  44.8 158.3 %copy-start.14 = (f32[8,128]{1,0:T(8,128)}, f32[8,128]{1,0:T(8,128)S(1)}, u32[]{:S(2)}) copy-start(f32[8,128]{1,0:T(8,128)S(1)} %fusion.18) | copy-start | bytes 12292
  44.8 79.7 %copy-start.5 = (s32[960]{0:T(1024)}, s32[960]{0:T(1024)S(1)}, u32[]{:S(2)}) copy-start(s32[960]{0:T(1024)S(1)} %fusion.44) | copy-start | bytes 11524
  44.9 79.7 %copy-start.7 = (f32[960]{0:T(1024)}, f32[960]{0:T(1024)S(1)}, u32[]{:S(2)}) copy-start(f32[960]{0:T(1024)S(1)} %convert_multiply_fusion) | copy-start | bytes 11524
  50.3 74.3 %copy-start.9 = (f32[960]{0:T(1024)}, f32[960]{0:T(1024)S(1)}, u32[]{:S(2)}) copy-start(f32[960]{0:T(1024)S(1)} %neg.24) | copy-start | bytes 11524
  53.5 149.7 %copy-start.2 = (f32[8,960]{1,0:T(8,128)}, f32[8,960]{1,0:T(8,128)S(1)}, u32[]{:S(2)}) copy-start(f32[8,960]{1,0:T(8,128)S(1)} %get-tuple-element.13) | copy-start | bytes 92164
  109.6 52.1 %copy-start.13 = (f32[8,128]{1,0:T(8,128)S(1)}, f32[8,128]{1,0:T(8,128)}, u32[]{:S(2)}) copy-start(f32[8,128]{1,0:T(8,128)} %param.25) | copy-start | bytes 12292
  116.1 3.1 %copy-start.1 = (f32[8,256,960]{1,2,0:T(8,128)}, f32[8,256,960]{1,2,0:T(8,128)S(1)}, u32[]{:S(2)}) copy-start(f32[8,256,960]{1,2,0:T(8,128)S(1)} %fusion.23) | copy-start | bytes 23592964
  161.6 41.5 %copy-start.11 = (f32[8,128]{1,0:T(8,128)}, f32[8,128]{1,0:T(8,128)S(1)}, u32[]{:S(2)}) copy-start(f32[8,128]{1,0:T(8,128)S(1)} %broadcast_multiply_fusion.1) | copy-start | bytes 12292
  203.2 0.6 copy-start.15
  210.6 6.7 %slice-start = ((s8[7864320]{0:T(1024)(128)(4,1)}), s8[4194304]{0:T(1024)(128)(4,1)S(1)}, s32[]{:S(2)}) async-start(s8[7864320]{0:T(1024)(128)(4,1)} %bitcast.189), calls=%async_computation | async-start | bytes 8388608
  210.8 6.5 %slice-start.1 = ((s8[7864320]{0:T(1024)(128)(4,1)}), s8[3670016]{0:T(1024)(128)(4,1)S(1)}, s32[]{:S(2)}) async-start(s8[7864320]{0:T(1024)(128)(4,1)} %bitcast.189), calls=%async_computation.1 | async-start | bytes 7340032
  210.8 6.5 %copy-start.3 = (f32[8,960]{1,0:T(8,128)S(1)}, f32[8,960]{1,0:T(8,128)}, u32[]{:S(2)}) copy-start(f32[8,960]{1,0:T(8,128)} %copy-done.2) | copy-start | bytes 92164
  210.8 6.5 %copy-start.4 = (f32[8,960]{1,0:T(8,128)S(1)}, f32[8,960]{1,0:T(8,128)}, u32[]{:S(2)}) copy-start(f32[8,960]{1,0:T(8,128)} %get-tuple-element.11) | copy-start | bytes 92164
  217.3 7.6 %copy-start.12 = (f32[32,256]{1,0:T(8,128)S(1)}, f32[32,256]{1,0:T(8,128)}, u32[]{:S(2)}) copy-start(f32[32,256]{1,0:T(8,128)} %param.15) | copy-start | bytes 98308
  217.3 8.3 %copy-start.6 = (s32[960]{0:T(1024)S(1)}, s32[960]{0:T(1024)}, u32[]{:S(2)}) copy-start(s32[960]{0:T(1024)} %copy-done.5) | copy-start | bytes 11524
  217.3 8.3 %copy-start.8 = (f32[960]{0:T(1024)S(1)}, f32[960]{0:T(1024)}, u32[]{:S(2)}) copy-start(f32[960]{0:T(1024)} %copy-done.7) | copy-start | bytes 11524
  217.3 8.3 %copy-start.10 = (f32[960]{0:T(1024)S(1)}, f32[960]{0:T(1024)}, u32[]{:S(2)}) copy-start(f32[960]{0:T(1024)} %copy-done.9) | copy-start | bytes 11524
  217.3 8.3 %copy-start.17 = (s32[8]{0:T(128)S(1)}, s32[8]{0:T(128)}, u32[]{:S(2)}) copy-start(s32[8]{0:T(128)} %copy-done.16) | copy-start | bytes 100
  217.4 8.3 %copy-start.19 = (f32[8]{0:T(128)S(1)}, f32[8]{0:T(128)}, u32[]{:S(2)}) copy-start(f32[8]{0:T(128)} %copy-done.18) | copy-start | bytes 100
where the time goes:
time: 272 us; the launch traced here: 271 us
  blocking collectives  201 us (74%)
  matrix products  42.6 us (16%)
  other arithmetic  17.4 us (6%)
  local copies, waits for them, and re-layouts  8.13 us (3%)
    all_gather x1, blocking collectives, per_device(): lax.all_gather(set_ids, 'path', axis=0, tiled=True)  41.9 us
    all_gather x1, blocking collectives, per_device(): lax.all_gather(live_flows, 'path', axis=0, tiled=True)  41.7 us
    psum x1, blocking collectives, per_device(): mean_slope = lax.psum(jnp.sum(slope, axis=2), 'path') / paths_all  41.2 us
    psum x1, blocking collectives, per_device(): rate_total = lax.psum(rate_adjoint, 'path')  39.6 us
    psum x1, blocking collectives, per_device(): mean_value = lax.psum(jnp.sum(values, axis=2), 'path') / paths_all  37 us
    unnamed x8, other arithmetic  12 us
    dot_general x1, matrix products, per_device(): jnp.einsum('fm,imp->ifp', factor_load, feat_adjoint * feat_exact * loadin...  7.57 us
    dot_general x1, matrix products, per_device(): shift = jnp.einsum('fm,ifp->imp', factor_load, states, precision=highest)  6.46 us

commit v1 on v0

--- a/solution.py
+++ b/solution.py
@@ -9,6 +9,18 @@
 HORIZON_YEARS = 30.0
 SHARPNESS = 4.0
 LOSS_RATE = 0.6
+
+
+def collect(shard, axis, dim):
+    ways, here = (lax.axis_size(axis), lax.axis_index(axis))
+    grown, reach = (shard, 1)
+    while reach < ways:
+        theirs = lax.ppermute(grown, axis, [(d, d ^ reach) for d in range(ways)])
+        mine_first = jnp.concatenate([grown, theirs], axis=dim)
+        theirs_first = jnp.concatenate([theirs, grown], axis=dim)
+        grown = jnp.where(here & reach == 0, mine_first, theirs_first)
+        reach = 2 * reach
+    return grown
 
 
 def curve_terms(knots, spline_jac, date_count, knot_count):
@@ -62,7 +74,7 @@
     set_ids = trade_set[:, 0]
     labels = jnp.arange(set_count, dtype=jnp.int32)
     all_flows, all_sets = (
-        lax.all_gather(live_flows, "path", axis=0, tiled=True),
+        collect(live_flows, "path", 0),
         lax.all_gather(set_ids, "path", axis=0, tiled=True),
     )
     member = (labels[:, None] == all_sets[None, :]).astype(jnp.bfloat16)

time: 272 us -> 258 us (0.949)
  blocking collectives: 201 us -> 160 us
  waiting for transfers between devices: 0 us -> 16.9 us
  starting transfers between devices: 0 us -> 8.76 us
  matrix products: 42.6 us -> 49.9 us
  local copies, waits for them, and re-layouts: 8.13 us -> 4.23 us
    all_gather x1 -> x0, blocking collectives: 41.7 us -> none  [per_device(): lax.all_gather(live_flows, 'path', axis=0, tiled=True)]
    ppermute x0 -> x5, waiting for transfers between devices: none -> 16.9 us  [collect(): theirs = lax.ppermute(grown, axis, [(d, d ^ reach) for d in range(ways)])]
    ppermute x0 -> x5, starting transfers between devices: none -> 8.76 us  [collect(): theirs = lax.ppermute(grown, axis, [(d, d ^ reach) for d in range(ways)])]
    unnamed x47 -> x9, local copies, waits for them, and re-layouts: 5.08 us -> 1.34 us
    dot_general x1, matrix products: 7.57 us -> 11 us  [per_device(): jnp.einsum('fm,imp->ifp', factor_load, feat_adjoint * feat_exact * loadin...]
    unnamed x8 -> x7, other arithmetic: 12 us -> 11.7 us
  transfers between devices with their start and end apart: 0 -> 5, of which waited for: 0 -> 4; matrix products, arithmetic and copies ran while one was open for 0% -> 12% of each run, Pallas kernels for 0% -> 0%
where the time goes in v1:
time: 258 us; the launch traced here: 257 us
  blocking collectives  160 us (62%)
  matrix products  49.9 us (19%)
  waiting for transfers between devices  16.9 us (7%)
  other arithmetic  16.1 us (6%)
  starting transfers between devices  8.76 us (3%)
  local copies, waits for them, and re-layouts  4.23 us (2%)
    psum x1, blocking collectives, per_device(): mean_slope = lax.psum(jnp.sum(slope, axis=2), 'path') / paths_all  42.3 us
    all_gather x1, blocking collectives, per_device(): lax.all_gather(set_ids, 'path', axis=0, tiled=True)  41.5 us
    psum x1, blocking collectives, per_device(): mean_value = lax.psum(jnp.sum(values, axis=2), 'path') / paths_all  38.3 us
    psum x1, blocking collectives, per_device(): rate_total = lax.psum(rate_adjoint, 'path')  38.1 us
    ppermute x5, waiting for transfers between devices, collect(): theirs = lax.ppermute(grown, axis, [(d, d ^ reach) for d in range(ways)])  16.9 us
    unnamed x7, other arithmetic  11.7 us
    dot_general x1, matrix products, per_device(): jnp.einsum('fm,imp->ifp', factor_load, feat_adjoint * feat_exact * loadin...  11 us
    ppermute x5, starting transfers between devices, collect(): theirs = lax.ppermute(grown, axis, [(d, d ^ reach) for d in range(ways)])  8.76 us
  transfers between devices with their start and end apart: 5, of which 4 were waited for; matrix products, arithmetic and copies ran while one was open for 12% of the time, Pallas kernels for 0%

profile of v1, /device:TPU:0, one launch (start us, length us, event | category | flops | bytes accessed | tf_op | source)
XLA Modules:
  0.0 256.8 jit_solution(3887648041533514649)
XLA Ops:
  0.6 0.0 copy-start
  0.6 0.8 fusion.42
  1.5 0.5 collective-permute-start
  2.0 0.7 bitcast_dynamic-update-slice_fusion.8
  2.7 41.5 %all-reduce = s32[256]{0:T(256)S(1)} all-reduce(s32[256]{0:T(256)S(1)} %bitcast_dynamic-update-slice_fusion.8), channel_id=2, replica_groups=mesh['group'=1,'path'=32] {'path'}, use_global_device_ids=true, to_apply=%add | all-reduce | flops 256 | bytes 2048 | tf_op jit(solution)/shard_map/all_gather | solution.py:78
  44.2 1.6 fusion.49
  45.8 0.8 fusion.18
  46.7 5.5 %fusion.51 = f32[1,960]{1,0:T(1,128)S(1)} fusion(f32[960,960]{1,0:T(8,128)} %param.19, f32[960,1]{0,1:T(1,128)} %bitcast.189), kind=kOutput, calls=%fused_computation.102 | convolution fusion | flops 11059200 | bytes 3694080 | tf_op jit(solution)/shard_map/dot_general | solution.py:27
  52.1 1.4 bitcast_dynamic-update-slice_fusion.7
  53.5 2.1 bitcast_dynamic-update-slice_fusion.6
  55.6 1.3 bitcast_dynamic-update-slice_fusion.5
  56.9 2.0 bitcast_dynamic-update-slice_fusion.4
  59.0 1.4 bitcast_dynamic-update-slice_fusion.3
  60.4 2.1 bitcast_dynamic-update-slice_fusion.2
  62.5 1.4 bitcast_dynamic-update-slice_fusion.1
  63.8 2.0 bitcast_dynamic-update-slice_fusion
  65.9 0.0 copy-done
  65.9 8.5 %fusion.23 = f32[8,256,960]{1,2,0:T(8,128)} fusion(f32[8,32,256]{2,1,0:T(8,128)S(1)} %bitcast_dynamic-update-slice_fusion, f32[32,960]{1,0:T(8,128)S(1)} %copy-done), kind=kOutput, calls=%fused_computation.31 | convolution fusion | flops 754974720 | bytes 8249344 | tf_op jit(solution)/shard_map/fm,ifp->imp/dot_general | solution.py:87
  74.4 0.0 copy-start.2
  74.4 0.0 collective-permute-done
  74.4 2.3 collective-permute-start.1
  76.8 1.9 collective-permute-done.1
  78.7 2.1 collective-permute-start.2
  80.8 2.2 collective-permute-done.2
  83.0 1.6 collective-permute-start.3
  84.6 5.0 %collective-permute-done.3 = bf16[64,960]{1,0:T(8,128)(2,1)S(1)} collective-permute-done((bf16[64,960]{1,0:T(8,128)(2,1)S(1)}, bf16[64,960]{1,0:T(8,128)(2,1)S(1)}, u32[]{:S(2)}, u32[]{:S(2)}) %collective-permute-start.3) | collective-permute-done | bytes 122912 | tf_op jit(solution)/shard_map/ppermute | solution.py:18
  89.6 0.1 maximum_select_fusion.1
  89.7 2.3 collective-permute-start.4
  91.9 0.1 subtract_multiply_fusion
  92.0 7.8 %collective-permute-done.4 = bf16[128,960]{1,0:T(8,128)(2,1)S(1)} collective-permute-done((bf16[128,960]{1,0:T(8,128)(2,1)S(1)}, bf16[128,960]{1,0:T(8,128)(2,1)S(1)}, u32[]{:S(2)}, u32[]{:S(2)}) %collective-permute-start.4) | collective-permute-done | bytes 245792 | tf_op jit(solution)/shard_map/ppermute | solution.py:18
  99.8 0.3 fusion.17
  100.1 6.6 %fusion.50 = (f32[8,128]{1,0:T(8,128)S(1)}, f32[8,128,256]{1,2,0:T(8,128)S(1)}) fusion(bf16[128,960,1]{0,1,2:T(8,128)(2,1)S(1)} %fusion.17, f32[8,256,960]{1,2,0:T(8,128)} %fusion.23, f32[8,960]{1,0:T(8,128)S(1)} %get-tuple-element.12, f32[8,960]{1,0:T(8,128)S(1)} %get-tuple-element.13), kind=kOutput, calls=%fused_computation.101 | convolution fusion | flops 509475840 | bytes 9224192 | tf_op jit(solution)/shard_map/nm,imp->inp/dot_general | solution.py:91
  106.7 38.3 %psum.21 = f32[8,128]{1,0:T(8,128)S(1)} all-reduce(f32[8,128]{1,0:T(8,128)S(1)} %get-tuple-element.22), channel_id=1, replica_groups=mesh['group'=1,'path'=32] {'path'}, use_global_device_ids=true, to_apply=%region_1.2 | all-reduce | flops 1024 | bytes 8192 | tf_op jit(solution)/shard_map/psum | solution.py:92
  145.1 0.0 copy-done.2
  145.1 0.3 fusion.48
  145.4 42.3 %psum.22 = f32[8,128]{1,0:T(8,128)S(1)} all-reduce(f32[8,128]{1,0:T(8,128)S(1)} %fusion.48), channel_id=1, replica_groups=mesh['group'=1,'path'=32] {'path'}, use_global_device_ids=true, to_apply=%region_3.4 | all-reduce | flops 1024 | bytes 8192 | tf_op jit(solution)/shard_map/psum | solution.py:95
  187.6 5.4 %fusion.10 = f32[128,960]{0,1:T(8,128)S(1)} fusion(f32[8,256,960]{1,2,0:T(8,128)} %fusion.23, f32[8,960]{1,0:T(8,128)S(1)} %get-tuple-element.12, f32[8,960]{1,0:T(8,128)S(1)} %get-tuple-element.13, f32[8,128]{1,0:T(8,128)S(1)} %broadcast_multiply_fusion, f32[8,128,256]{1,2,0:T(8,128)S(1)} %get-tuple-element.23, f32[8,128]{1,0:T(8,128)S(1)} %copy-done.2, ...), kind=kOutput, calls=%fused_computation.16 | convolution fusion | flops 511696896 | bytes 9482240 | tf_op jit(solution)/shard_map/inp,imp->nm/dot_general | solution.py:111
  193.1 7.1 %fusion = (f32[8,960]{1,0:T(8,128)S(1)}, f32[8,256,960]{1,2,0:T(8,128)}) fusion(f32[8,256,960]{1,2,0:T(8,128)} %fusion.23, f32[8,960]{1,0:T(8,128)S(1)} %get-tuple-element.12, bf16[128,960,1]{0,1,2:T(8,128)(2,1)S(1)} %fusion.17, f32[8,128]{1,0:T(8,128)S(1)} %broadcast_multiply_fusion, f32[8,128]{1,0:T(8,128)S(1)} %copy-done.2, ...), kind=kOutput, calls=%fused_computation.3 | convolution fusion | flops 511566336 | bytes 17100800 | tf_op jit(solution)/shard_map/nm,inp->imp/dot_general | solution.py:97
  200.1 0.2 copy.21
  200.3 0.1 multiply_reduce_fusion.1
  200.4 1.1 gather_fusion
  201.5 0.2 multiply_reduce_fusion
  201.7 38.1 %all-reduce.2 = (f32[960]{0:T(1024)S(1)}, f32[256]{0:T(256)S(1)}) all-reduce(f32[960]{0:T(1024)S(1)} %negate_multiply_fusion, f32[256]{0:T(256)S(1)} %multiply_reduce_fusion), channel_id=1, replica_groups=mesh['group'=1,'path'=32] {'path'}, use_global_device_ids=true, to_apply=%region_6.7 | all-reduce | flops 1216 | bytes 9728 | tf_op jit(solution)/shard_map/psum | solution.py:108
  239.9 4.7 %fusion.5 = f32[1,960]{1,0:T(1,128)} fusion(f32[960,1]{0,1:T(1,128)S(1)} %bitcast.191, f32[960,960]{1,0:T(8,128)} %param.19), kind=kOutput, calls=%fused_computation.9 | convolution fusion | flops 11059200 | bytes 3694080 | tf_op jit(solution)/shard_map/dot_general | solution.py:109
  244.5 11.0 %fusion.14 = f32[8,32,256]{2,1,0:T(8,128)S(1)} fusion(f32[8,256,960]{1,2,0:T(8,128)} %get-tuple-element.25, f32[8,256,960]{1,2,0:T(8,128)} %fusion.23, f32[8,960]{1,0:T(8,128)S(1)} %get-tuple-element.11, f32[8,960]{1,0:T(8,128)S(1)} %get-tuple-element.12, f32[8,960]{1,0:T(8,128)S(1)} %get-tuple-element.13, f32[32,960]{1,0:T(8,128)S(1)} %copy-done), kind=kOutput, calls=%fused_computation.19 | convolution fusion | flops 762904576 | bytes 16205824 | tf_op jit(solution)/shard_map/fm,imp->ifp/dot_general | solution.py:100
  255.6 0.0 copy-done.1
  255.6 0.6 fusion.41
  256.2 0.6 dynamic-slice
  (15 shorter events, 0.1 us)
Async XLA Ops:
  0.6 65.3 %copy-start = (f32[32,960]{1,0:T(8,128)S(1)}, f32[32,960]{1,0:T(8,128)}, u32[]{:S(2)}) copy-start(f32[32,960]{1,0:T(8,128)} %param.17) | copy-start | bytes 368644
  1.5 72.9 %collective-permute-start = (bf16[8,960]{1,0:T(8,128)(2,1)S(1)}, bf16[8,960]{1,0:T(8,128)(2,1)S(1)}, u32[]{:S(2)}, u32[]{:S(2)}) collective-permute-start(bf16[8,960]{1,0:T(8,128)(2,1)S(1)} %fusion.42), channel_id=1, source_target_pairs={{0,1},{1,0},{2,3},{3,2},{4,5},{5,4},{6,7},{7,6},{8,9},{9,8},{10,11... | collective-permute-start | bytes 46088 | tf_op jit(solution)/shard_map/ppermute | solution.py:18
  74.4 70.7 %copy-start.2 = (f32[8,128]{1,0:T(8,128)S(1)}, f32[8,128]{1,0:T(8,128)}, u32[]{:S(2)}) copy-start(f32[8,128]{1,0:T(8,128)} %param.25) | copy-start | bytes 12292
  74.4 4.2 %collective-permute-start.1 = (bf16[16,960]{1,0:T(8,128)(2,1)S(1)}, bf16[16,960]{1,0:T(8,128)(2,1)S(1)}, u32[]{:S(2)}, u32[]{:S(2)}) collective-permute-start(bf16[16,960]{1,0:T(8,128)(2,1)S(1)} %maximum_select_fusion.5), channel_id=1, source_target_pairs={{0,2},{1,3},{2,0},{3,1},{4,6},{5,7},{6,4},{7,5},{8,10},{9,11},{10,... | collective-permute-start | bytes 92168 | tf_op jit(solution)/shard_map/ppermute | solution.py:18
  78.7 4.3 %collective-permute-start.2 = (bf16[32,960]{1,0:T(8,128)(2,1)S(1)}, bf16[32,960]{1,0:T(8,128)(2,1)S(1)}, u32[]{:S(2)}, u32[]{:S(2)}) collective-permute-start(bf16[32,960]{1,0:T(8,128)(2,1)S(1)} %maximum_select_fusion.4), channel_id=1, source_target_pairs={{0,4},{1,5},{2,6},{3,7},{4,0},{5,1},{6,2},{7,3},{8,12},{9,13},{10,... | collective-permute-start | bytes 184328 | tf_op jit(solution)/shard_map/ppermute | solution.py:18
  83.0 6.6 %collective-permute-start.3 = (bf16[64,960]{1,0:T(8,128)(2,1)S(1)}, bf16[64,960]{1,0:T(8,128)(2,1)S(1)}, u32[]{:S(2)}, u32[]{:S(2)}) collective-permute-start(bf16[64,960]{1,0:T(8,128)(2,1)S(1)} %maximum_select_fusion.2), channel_id=1, source_target_pairs={{0,8},{1,9},{2,10},{3,11},{4,12},{5,13},{6,14},{7,15},{8,0},{9,1},... | collective-permute-start | bytes 368648 | tf_op jit(solution)/shard_map/ppermute | solution.py:18
  89.7 10.1 %collective-permute-start.4 = (bf16[128,960]{1,0:T(8,128)(2,1)S(1)}, bf16[128,960]{1,0:T(8,128)(2,1)S(1)}, u32[]{:S(2)}, u32[]{:S(2)}) collective-permute-start(bf16[128,960]{1,0:T(8,128)(2,1)S(1)} %maximum_select_fusion.1), channel_id=1, source_target_pairs={{0,16},{1,17},{2,18},{3,19},{4,20},{5,21},{6,22},{7,23},{8,24},{9,... | collective-permute-start | bytes 737288 | tf_op jit(solution)/shard_map/ppermute | solution.py:18
  244.5 11.1 %copy-start.1 = (f32[32,256]{1,0:T(8,128)S(1)}, f32[32,256]{1,0:T(8,128)}, u32[]{:S(2)}) copy-start(f32[32,256]{1,0:T(8,128)} %param.15) | copy-start | bytes 98308
